TPU v7x, 512 devices: a whole 4x8x8 slice. The times are simulated.
512 devices in a mesh: dp: 64 (over z, y_hi, core), mp: 8 (over y_lo, x).
Axes of the slice: x: 4, y: 8 (y_hi: 4, y_lo: 2; y = y_hi * 2 + y_lo), z: 8, core: 2. Of those that a mesh axis runs over, the one named last changes fastest.
Arguments:
- views: bfloat16 [32768, 256], P('dp'), may hold values from -1 to 1
- partner: int32 [32768], P('dp'), may hold values from 0 to 32767, as said below
- weight: float32 [32768], P('dp'), may hold values from 0.25 to 4
Outputs:
- loss: float32 [32768], P('dp')
- grad: float32 [32768, 256], P('dp')
Inputs may be any that keep to these rules, and one draw needn't show every extreme that they name: partner pairs the views: partner[partner[i]] = i and partner[i] != i.
All inputs are finite; a program needn't handle non-finite values.
Results may differ from a plain program's by a relative error of at most 0.0056.
Values may be sent and summed in bfloat16 or wider, within the bound.
No kernel may reach another device: no remote copies, remote signals or barrier semaphores. Data moves between devices by JAX's collectives and lax.ppermute only.
A program may use at most 64 MiB of HBM per device.

v0:
```python
import jax
import jax.numpy as jnp
from jax import lax
from jax.sharding import Mesh
from jax.sharding import PartitionSpec as P

DP = ("dp_0", "dp_1", "dp_2")
INV_TAU = 10.0
EPS = 1e-06


def sent_to_all(shard, axis):
    count = lax.axis_size(axis)
    return lax.all_to_all(
        jnp.broadcast_to(shard[None], (count, *shard.shape)), axis, 0, 0, tiled=True
    )


def joined_along(parts, dim):
    parts = jnp.moveaxis(parts, 0, dim)
    shape = parts.shape
    return parts.reshape(*shape[:dim], shape[dim] * shape[dim + 1], *shape[dim + 2 :])


def gathered_by_axis(shard, axes, dim):
    far, near = axes
    leading = sent_to_all(shard, far)
    parts = jnp.swapaxes(sent_to_all(leading, near), 0, 1)
    return joined_along(parts.reshape(-1, *shard.shape), dim)


def of_everyone(shard, axis):
    everything = sent_to_all(shard, axis)
    return jnp.sum(everything, axis=0)


def together(arrays, axis):
    vector, at, finished = (jnp.concatenate([a.reshape(-1) for a in arrays]), 0, [])
    subtotal = of_everyone(vector, axis)
    for a in arrays:
        finished.append(subtotal[at : at + a.size].reshape(a.shape))
        at += a.size
    return tuple(finished)


def turned_gather(arrays, axis, dims):
    turned = [jnp.moveaxis(a, dim, 0) for a, dim in zip(arrays, dims)]
    widths = [t[0].size for t in turned]
    both = jnp.concatenate([t.reshape(-1, w) for t, w in zip(turned, widths)], axis=1)
    whole = lax.all_gather(both, axis, axis=0, tiled=True)
    parts = jnp.split(whole, [sum(widths[:k]) for k in range(1, len(widths))], axis=1)
    return tuple(
        (
            jnp.moveaxis(b.reshape(-1, *t.shape[1:]), 0, dim)
            for b, t, dim in zip(parts, turned, dims)
        )
    )


def cut_along(shard, dim, count):
    shape = shard.shape
    parts = shard.reshape(*shape[:dim], count, shape[dim] // count, *shape[dim + 1 :])
    return jnp.moveaxis(parts, dim, 0)


def sent_and_summed(shard, axis, dim):
    parts = cut_along(shard, dim, lax.axis_size(axis))
    arrived = lax.all_to_all(parts, axis, split_axis=0, concat_axis=0, tiled=True)
    return arrived.sum(axis=0)


def gather_directly(shard, axis, dim):
    parts = sent_to_all(shard, axis)
    return joined_along(parts, dim)


def shards(views, partner, weight):
    rows_dev = views.shape[0]
    width = views.shape[1]
    parts = lax.axis_size("mp")
    slot = lax.axis_index("mp")
    block_index = lax.axis_index(DP)
    piece = rows_dev // parts
    floats = views.astype(jnp.float32)
    length = jnp.sqrt(jnp.sum(floats * floats, axis=1) + EPS)
    unit = floats / length[:, None]
    normal = unit.astype(jnp.bfloat16)
    offset = slot * piece
    mine = lax.dynamic_slice_in_dim(normal, offset, piece, 0)
    columns = gathered_by_axis(mine, (("dp_0", "dp_1"), "dp_2"), 0)
    width_cols = columns.shape[0]
    step_cols = min(512, width_cols)
    count = width_cols // step_cols
    position = jnp.arange(width_cols, dtype=jnp.int32)
    col_ids = position // piece * rows_dev + offset + position % piece
    row_ids = block_index * rows_dev + jnp.arange(rows_dev, dtype=jnp.int32)
    id_blocks = col_ids.reshape(count, step_cols)

    def tile(cols_block, ids_block):
        s = (
            lax.dot_general(
                normal, cols_block, (((1,), (1,)), ((), ())), preferred_element_type=jnp.float32
            )
            * INV_TAU
        )
        off = row_ids[:, None] != ids_block[None, :]
        match = partner[:, None] == ids_block[None, :]
        return (s, off, match)

    def forward(carry, inputs):
        cols_block, ids_block = inputs
        s, off, match = tile(cols_block, ids_block)
        total = carry[0] + jnp.sum(jnp.where(off, jnp.exp(s), jnp.float32(0.0)), axis=1)
        positive = carry[1] + jnp.sum(jnp.where(match, s, jnp.float32(0.0)), axis=1)
        return ((total, positive), None)

    zeros_rows = jnp.zeros((rows_dev,), jnp.float32)
    col_blocks = columns.reshape(count, step_cols, width)
    (total, positive), _ = lax.scan(forward, (zeros_rows, zeros_rows), (col_blocks, id_blocks))
    total, positive = together((total, positive), "mp")
    lse = jnp.log(total)
    loss = lse - positive
    lse_mine = lax.dynamic_slice_in_dim(lse, offset, piece, 0)
    weight_mine = lax.dynamic_slice_in_dim(weight, offset, piece, 0)
    col_lse, col_weight = turned_gather((lse_mine, weight_mine), DP, (0, 0))

    def backward(acc, inputs):
        cols_block, ids_block, lse_block, weight_block = inputs
        s, off, match = tile(cols_block, ids_block)
        prow = jnp.exp(s - lse[:, None])
        pcol = jnp.exp(s - lse_block[None, :])
        coef = jnp.where(
            off, weight[:, None] * prow + weight_block[None, :] * pcol, jnp.float32(0.0)
        )
        coef = coef - jnp.where(match, weight[:, None] + weight_block[None, :], jnp.float32(0.0))
        coef = coef.astype(jnp.bfloat16)
        return (acc + jnp.dot(coef, cols_block, preferred_element_type=jnp.float32), None)

    start_acc = jnp.zeros((rows_dev, width), jnp.float32)
    partial_grad, _ = lax.scan(
        backward,
        start_acc,
        (
            col_blocks,
            id_blocks,
            col_lse.reshape(count, step_cols),
            col_weight.reshape(count, step_cols),
        ),
    )
    share = sent_and_summed(partial_grad, "mp", 0) * INV_TAU
    unit_share = lax.dynamic_slice_in_dim(unit, offset, piece, 0)
    length_share = lax.dynamic_slice_in_dim(length, offset, piece, 0)
    finished = (
        share - unit_share * jnp.sum(unit_share * share, axis=1, keepdims=True)
    ) / length_share[:, None]
    grad = gather_directly(finished, "mp", 0)
    return (loss, grad)


def solution(mesh):
    finer = Mesh(mesh.devices.reshape(8, 4, 2, mesh.shape["mp"]), ("dp_0", "dp_1", "dp_2", "mp"))
    placed = (P(DP, None), P(DP), P(DP))
    return jax.shard_map(
        shards, mesh=finer, in_specs=placed, out_specs=(P(DP), P(DP, None)), check_vma=False
    )
```

profile of v0, /device:TPU:1, one launch (start us, length us, event | category | flops | bytes accessed | tf_op | source)
XLA Modules:
  0.0 204.9 jit_solution(12894335910544377624)
XLA Ops:
  0.6 1.1 fusion.31
  1.7 1.1 convert_divide_fusion
  2.9 1.1 broadcast_in_dim.26
  4.0 16.5 %all-to-all-start = ((bf16[32,64,256]{2,1,0:T(8,128)(2,1)}), bf16[32,64,256]{2,1,0:T(8,128)(2,1)S(1)}, u32[]{:S(2)}, u32[]{:S(2)}) async-start(bf16[32,64,256]{2,1,0:T(8,128)(2,1)} %broadcast_in_dim.26), calls=%async_computation | async-start | bytes 2097152 | tf_op jit(solution)/shard_map/all_to_all | solution.py:14
  20.6 31.4 %all-to-all-done = bf16[32,64,256]{2,1,0:T(8,128)(2,1)S(1)} async-done(((bf16[32,64,256]{2,1,0:T(8,128)(2,1)}), bf16[32,64,256]{2,1,0:T(8,128)(2,1)S(1)}, u32[]{:S(2)}, u32[]{:S(2)}) %all-to-all-start) | async-done | bytes 1048608 | tf_op jit(solution)/shard_map/all_to_all | solution.py:14
  51.9 0.2 broadcast_in_dim.27
  52.2 8.1 %all_to_all.26 = bf16[2,32,64,256]{3,2,1,0:T(8,128)(2,1)S(1)} all-to-all(bf16[2,32,64,256]{3,2,1,0:T(8,128)(2,1)S(1)} %broadcast_in_dim.27), channel_id=1, replica_groups=mesh['dp_0'=8,'dp_1'=4,'dp_2'=2,'mp'=8] {'dp_2'}, dimensions={0} | all-to-all | bytes 4194304 | tf_op jit(solution)/shard_map/all_to_all | solution.py:14
  60.3 0.0 copy-start
  60.3 0.1 copy.11
  60.4 0.5 copy-done
  61.0 0.0 copy-start.1
  61.0 4.7 %while.24 = (s32[]{:T(128)}, f32[512]{0:T(512)S(1)}, f32[512]{0:T(512)S(1)}, s32[8,512]{1,0:T(8,128)S(1)}, bf16[8,512,256]{2,1,0:T(8,128)(2,1)S(1)}, /*index=5*/...) while((s32[]{:T(128)}, f32[512]{0:T(512)S(1)}, ...), condition=%wide.region_4.5_spmd.clone, body=%wide.region_1.4_spmd.clone.sunk | while | flops 136054272 | bytes 553083 | solution.py:119
  61.0 0.5 select_reduce_fusion.3
  61.6 0.5 select_reduce_fusion.3
  62.2 0.5 select_reduce_fusion.3
  62.8 0.5 select_reduce_fusion.3
  63.3 0.5 select_reduce_fusion.3
  63.9 0.5 select_reduce_fusion.3
  64.5 0.5 select_reduce_fusion.3
  65.1 0.5 select_reduce_fusion.3
  65.7 0.6 broadcast_in_dim.28
  66.3 4.0 %all-to-all-start.2 = ((f32[8,1,1024]{2,1,0:T(1,128)}), f32[8,1,1024]{2,1,0:T(1,128)S(1)}, u32[]{:S(2)}, u32[]{:S(2)}) async-start(f32[8,1,1024]{2,1,0:T(1,128)} %broadcast_in_dim.28), calls=%async_computation.2 | async-start | bytes 65536 | tf_op jit(solution)/shard_map/all_to_all | solution.py:14
  70.3 0.0 copy-done.1
  70.3 0.1 dynamic-slice_bitcast_fusion
  70.4 5.0 %all-to-all-done.2 = f32[8,1,1024]{2,1,0:T(1,128)S(1)} async-done(((f32[8,1,1024]{2,1,0:T(1,128)}), f32[8,1,1024]{2,1,0:T(1,128)S(1)}, u32[]{:S(2)}, u32[]{:S(2)}) %all-to-all-start.2) | async-done | bytes 32800 | tf_op jit(solution)/shard_map/all_to_all | solution.py:14
  75.5 0.6 slice_log_fusion
  76.0 0.1 dynamic-slice_bitcast_fusion.1
  76.1 80.5 %all-gather = f32[64,64,2]{1,2,0:T(2,128)S(1)} all-gather(f32[1,64,2]{1,2,0:T(2,128)S(1)} %maximum_bitcast_fusion), channel_id=1, replica_groups=mesh['dp_0'=8,'dp_1'=4,'dp_2'=2,'mp'=8] {'dp_0','dp_1','dp_2'}, dimensions={0}, use_global_device_ids=true | all-gather | bytes 33280 | tf_op jit(solution)/shard_map/all_gather | solution.py:50
  156.7 0.1 reshape.51
  156.8 0.1 slice_reduce_fusion
  156.9 22.0 %while.25 = (s32[]{:T(128)}, f32[512,256]{1,0:T(8,128)}, s32[8,512]{1,0:T(8,128)S(1)}, f32[512]{0:T(512)S(1)}, bf16[8,512,256]{2,1,0:T(8,128)(2,1)S(1)}, /*index...) while((s32[]{:T(128)}, f32[512,256]{1,0:T(8,128)}, ...), condition=%wide.region_7.8_spmd.clone, body=%wide.region_6.7_spmd.clone.sunk | while | flops 272105984 | bytes 1868947 | solution.py:140
  156.9 1.8 convolution_add_fusion.2
  158.8 2.8 %convolution_add_fusion.2 = f32[512,256]{1,0:T(8,128)} fusion(bf16[512,256]{1,0:T(8,128)(2,1)S(1)} %get-tuple-element.413, f32[512,256]{1,0:T(8,128)} %get-tuple-element.396, f32[512]{0:T(512)S(1)} %bitcast.61, f32[512]{0:T(512)S(1)} %get-tuple-element.411, s32[512]{0:T(512)S(1)} %get-tuple-element.417, f32[512]{0:T(512)S(1)} %bitcast.60, ...), kind=kOutput, calls=%fused_computation.14.clone.1 | convolution fusion | flops 272105472 | bytes 1854465 | tf_op jit(solution)/shard_map/while/body/eval_jaxpr/dot_general | solution.py:137
  161.7 2.8 %convolution_add_fusion.2 = f32[512,256]{1,0:T(8,128)} fusion(bf16[512,256]{1,0:T(8,128)(2,1)S(1)} %get-tuple-element.413, f32[512,256]{1,0:T(8,128)} %get-tuple-element.396, f32[512]{0:T(512)S(1)} %bitcast.61, f32[512]{0:T(512)S(1)} %get-tuple-element.411, s32[512]{0:T(512)S(1)} %get-tuple-element.417, f32[512]{0:T(512)S(1)} %bitcast.60, ...), kind=kOutput, calls=%fused_computation.14.clone.1 | convolution fusion | flops 272105472 | bytes 1854465 | tf_op jit(solution)/shard_map/while/body/eval_jaxpr/dot_general | solution.py:137
  164.5 2.8 %convolution_add_fusion.2 = f32[512,256]{1,0:T(8,128)} fusion(bf16[512,256]{1,0:T(8,128)(2,1)S(1)} %get-tuple-element.413, f32[512,256]{1,0:T(8,128)} %get-tuple-element.396, f32[512]{0:T(512)S(1)} %bitcast.61, f32[512]{0:T(512)S(1)} %get-tuple-element.411, s32[512]{0:T(512)S(1)} %get-tuple-element.417, f32[512]{0:T(512)S(1)} %bitcast.60, ...), kind=kOutput, calls=%fused_computation.14.clone.1 | convolution fusion | flops 272105472 | bytes 1854465 | tf_op jit(solution)/shard_map/while/body/eval_jaxpr/dot_general | solution.py:137
  167.4 2.8 %convolution_add_fusion.2 = f32[512,256]{1,0:T(8,128)} fusion(bf16[512,256]{1,0:T(8,128)(2,1)S(1)} %get-tuple-element.413, f32[512,256]{1,0:T(8,128)} %get-tuple-element.396, f32[512]{0:T(512)S(1)} %bitcast.61, f32[512]{0:T(512)S(1)} %get-tuple-element.411, s32[512]{0:T(512)S(1)} %get-tuple-element.417, f32[512]{0:T(512)S(1)} %bitcast.60, ...), kind=kOutput, calls=%fused_computation.14.clone.1 | convolution fusion | flops 272105472 | bytes 1854465 | tf_op jit(solution)/shard_map/while/body/eval_jaxpr/dot_general | solution.py:137
  170.3 2.8 %convolution_add_fusion.2 = f32[512,256]{1,0:T(8,128)} fusion(bf16[512,256]{1,0:T(8,128)(2,1)S(1)} %get-tuple-element.413, f32[512,256]{1,0:T(8,128)} %get-tuple-element.396, f32[512]{0:T(512)S(1)} %bitcast.61, f32[512]{0:T(512)S(1)} %get-tuple-element.411, s32[512]{0:T(512)S(1)} %get-tuple-element.417, f32[512]{0:T(512)S(1)} %bitcast.60, ...), kind=kOutput, calls=%fused_computation.14.clone.1 | convolution fusion | flops 272105472 | bytes 1854465 | tf_op jit(solution)/shard_map/while/body/eval_jaxpr/dot_general | solution.py:137
  173.2 2.8 %convolution_add_fusion.2 = f32[512,256]{1,0:T(8,128)} fusion(bf16[512,256]{1,0:T(8,128)(2,1)S(1)} %get-tuple-element.413, f32[512,256]{1,0:T(8,128)} %get-tuple-element.396, f32[512]{0:T(512)S(1)} %bitcast.61, f32[512]{0:T(512)S(1)} %get-tuple-element.411, s32[512]{0:T(512)S(1)} %get-tuple-element.417, f32[512]{0:T(512)S(1)} %bitcast.60, ...), kind=kOutput, calls=%fused_computation.14.clone.1 | convolution fusion | flops 272105472 | bytes 1854465 | tf_op jit(solution)/shard_map/while/body/eval_jaxpr/dot_general | solution.py:137
  176.0 2.8 %convolution_add_fusion.2 = f32[512,256]{1,0:T(8,128)} fusion(bf16[512,256]{1,0:T(8,128)(2,1)S(1)} %get-tuple-element.413, f32[512,256]{1,0:T(8,128)} %get-tuple-element.396, f32[512]{0:T(512)S(1)} %bitcast.61, f32[512]{0:T(512)S(1)} %get-tuple-element.411, s32[512]{0:T(512)S(1)} %get-tuple-element.417, f32[512]{0:T(512)S(1)} %bitcast.60, ...), kind=kOutput, calls=%fused_computation.14.clone.1 | convolution fusion | flops 272105472 | bytes 1854465 | tf_op jit(solution)/shard_map/while/body/eval_jaxpr/dot_general | solution.py:137
  178.9 3.5 %all-to-all-start.3 = ((f32[8,64,256]{2,1,0:T(8,128)}), f32[8,64,256]{2,1,0:T(8,128)S(1)}, u32[]{:S(2)}, u32[]{:S(2)}) async-start(f32[8,64,256]{2,1,0:T(8,128)} %bitcast.6), calls=%async_computation.3 | async-start | bytes 1048576 | tf_op jit(solution)/shard_map/all_to_all | solution.py:68
  182.4 0.1 dynamic_slice.40
  182.4 8.5 %all-to-all-done.3 = f32[8,64,256]{2,1,0:T(8,128)S(1)} async-done(((f32[8,64,256]{2,1,0:T(8,128)}), f32[8,64,256]{2,1,0:T(8,128)S(1)}, u32[]{:S(2)}, u32[]{:S(2)}) %all-to-all-start.3) | async-done | bytes 524320 | tf_op jit(solution)/shard_map/all_to_all | solution.py:68
  191.0 0.1 multiply_reduce_fusion
  191.1 0.1 subtract_divide_fusion
  191.3 12.9 %all_to_all.27 = f32[8,64,256]{2,1,0:T(8,128)S(1)} all-to-all(f32[8,64,256]{2,1,0:T(8,128)S(1)} %broadcast_in_dim.30), channel_id=1, replica_groups=mesh['dp_0'=8,'dp_1'=4,'dp_2'=2,'mp'=8] {'mp'}, dimensions={0} | all-to-all | bytes 1048576 | tf_op jit(solution)/shard_map/all_to_all | solution.py:14
  204.1 0.8 copy.33
  (62 shorter events, 0.6 us)
Async XLA Ops:
  4.0 48.0 %all-to-all-start = ((bf16[32,64,256]{2,1,0:T(8,128)(2,1)}), bf16[32,64,256]{2,1,0:T(8,128)(2,1)S(1)}, u32[]{:S(2)}, u32[]{:S(2)}) async-start(bf16[32,64,256]{2,1,0:T(8,128)(2,1)} %broadcast_in_dim.26), calls=%async_computation | async-start | bytes 2097152 | tf_op jit(solution)/shard_map/all_to_all | solution.py:14
  60.3 0.7 copy-start
  61.0 9.4 %copy-start.1 = (f32[512]{0:T(512)S(1)}, f32[512]{0:T(512)}, u32[]{:S(2)}) copy-start(f32[512]{0:T(512)} %param.9) | copy-start | bytes 6148
  66.3 9.1 %all-to-all-start.2 = ((f32[8,1,1024]{2,1,0:T(1,128)}), f32[8,1,1024]{2,1,0:T(1,128)S(1)}, u32[]{:S(2)}, u32[]{:S(2)}) async-start(f32[8,1,1024]{2,1,0:T(1,128)} %broadcast_in_dim.28), calls=%async_computation.2 | async-start | bytes 65536 | tf_op jit(solution)/shard_map/all_to_all | solution.py:14
  178.9 12.1 %all-to-all-start.3 = ((f32[8,64,256]{2,1,0:T(8,128)}), f32[8,64,256]{2,1,0:T(8,128)S(1)}, u32[]{:S(2)}, u32[]{:S(2)}) async-start(f32[8,64,256]{2,1,0:T(8,128)} %bitcast.6), calls=%async_computation.3 | async-start | bytes 1048576 | tf_op jit(solution)/shard_map/all_to_all | solution.py:68
where the time goes:
time: 206 us; the launch traced here: 205 us
  blocking collectives  101 us (49%)
  waiting for transfers between devices  44.9 us (22%)
  matrix products  25.8 us (13%)
  starting transfers between devices  24 us (12%)
  local copies, waits for them, and re-layouts  4.12 us (2%)
  other arithmetic  3.33 us (2%)
    all_gather x1, blocking collectives, turned_gather(): whole = lax.all_gather(both, axis, axis=0, tiled=True)  80.5 us
    all_to_all x2, waiting for transfers between devices, sent_to_all(): lax.all_to_all(jnp.broadcast_to(shard[None], (count, *shard.shape)), axis...  36.4 us
    dot_general x8, matrix products, backward(): jnp.dot(coef, cols_block, preferred_element_type=jnp.float32)  21.6 us
    all_to_all x2, blocking collectives, sent_to_all(): lax.all_to_all(jnp.broadcast_to(shard[None], (count, *shard.shape)), axis...  21 us
    all_to_all x2, starting transfers between devices, sent_to_all(): lax.all_to_all(jnp.broadcast_to(shard[None], (count, *shard.shape)), axis...  20.5 us
    all_to_all x1, waiting for transfers between devices, sent_and_summed(): lax.all_to_all(parts, axis, split_axis=0, concat_axis=0, tiled=True)  8.51 us
    dot_general x8, matrix products, tile(): lax.dot_general(normal, cols_block, (((1,), (1,)), ((), ())), preferred_e...  4.18 us
  transfers between devices with their start and end apart: 3, of which 3 were waited for; matrix products, arithmetic and copies ran while one was open for 0% of the time, Pallas kernels for 0%

commit v1 on v0

--- a/solution.py
+++ b/solution.py
@@ -47,7 +47,9 @@
     turned = [jnp.moveaxis(a, dim, 0) for a, dim in zip(arrays, dims)]
     widths = [t[0].size for t in turned]
     both = jnp.concatenate([t.reshape(-1, w) for t, w in zip(turned, widths)], axis=1)
-    whole = lax.all_gather(both, axis, axis=0, tiled=True)
+    whole = jnp.concatenate(
+        lax.all_to_all(jnp.stack([both] * lax.axis_size(axis)), axis, 0, 0), axis=0
+    )
     parts = jnp.split(whole, [sum(widths[:k]) for k in range(1, len(widths))], axis=1)
     return tuple(
         (

time: 206 us -> 147 us (0.71)
  blocking collectives: 101 us -> 21.3 us
  waiting for transfers between devices: 44.9 us -> 56.3 us
  starting transfers between devices: 24 us -> 32.1 us
    all_gather x1 -> x0, blocking collectives: 80.5 us -> none  [turned_gather(): whole = lax.all_gather(both, axis, axis=0, tiled=True)]
    all_to_all x0 -> x1, waiting for transfers between devices: none -> 11.8 us  [turned_gather(): lax.all_to_all(jnp.stack([both] * lax.axis_size(axis)), axis, 0, 0)]
    all_to_all x0 -> x1, starting transfers between devices: none -> 8.05 us  [turned_gather(): lax.all_to_all(jnp.stack([both] * lax.axis_size(axis)), axis, 0, 0)]
  transfers between devices with their start and end apart: 3 -> 4, of which waited for: 3 -> 4; matrix products, arithmetic and copies ran while one was open for 0% -> 0% of each run, Pallas kernels for 0% -> 0%
where the time goes in v1:
time: 147 us; the launch traced here: 146 us
  waiting for transfers between devices  56.3 us (38%)
  starting transfers between devices  32.1 us (22%)
  matrix products  25.7 us (17%)
  blocking collectives  21.3 us (14%)
  local copies, waits for them, and re-layouts  5.56 us (4%)
  other arithmetic  4.09 us (3%)
    all_to_all x2, waiting for transfers between devices, sent_to_all(): lax.all_to_all(jnp.broadcast_to(shard[None], (count, *shard.shape)), axis...  36.4 us
    dot_general x8, matrix products, backward(): jnp.dot(coef, cols_block, preferred_element_type=jnp.float32)  21.6 us
    all_to_all x2, blocking collectives, sent_to_all(): lax.all_to_all(jnp.broadcast_to(shard[None], (count, *shard.shape)), axis...  21.3 us
    all_to_all x2, starting transfers between devices, sent_to_all(): lax.all_to_all(jnp.broadcast_to(shard[None], (count, *shard.shape)), axis...  20.5 us
    all_to_all x1, waiting for transfers between devices, turned_gather(): lax.all_to_all(jnp.stack([both] * lax.axis_size(axis)), axis, 0, 0)  11.8 us
    all_to_all x1, waiting for transfers between devices, sent_and_summed(): lax.all_to_all(parts, axis, split_axis=0, concat_axis=0, tiled=True)  8.07 us
    all_to_all x1, starting transfers between devices, turned_gather(): lax.all_to_all(jnp.stack([both] * lax.axis_size(axis)), axis, 0, 0)  8.05 us
    dot_general x8, matrix products, tile(): lax.dot_general(normal, cols_block, (((1,), (1,)), ((), ())), preferred_e...  4.18 us
  transfers between devices with their start and end apart: 4, of which 4 were waited for; matrix products, arithmetic and copies ran while one was open for 0% of the time, Pallas kernels for 0%

profile of v1, /device:TPU:1, one launch (start us, length us, event | category | flops | bytes accessed | tf_op | source)
XLA Modules:
  0.0 146.4 jit_solution(4092966686326012875)
XLA Ops:
  0.6 1.1 fusion.31
  1.7 1.1 convert_divide_fusion
  2.9 1.1 broadcast_in_dim.26
  4.0 16.5 %all-to-all-start = ((bf16[32,64,256]{2,1,0:T(8,128)(2,1)}), bf16[32,64,256]{2,1,0:T(8,128)(2,1)S(1)}, u32[]{:S(2)}, u32[]{:S(2)}) async-start(bf16[32,64,256]{2,1,0:T(8,128)(2,1)} %broadcast_in_dim.26), calls=%async_computation | async-start | bytes 2097152 | tf_op jit(solution)/shard_map/all_to_all | solution.py:14
  20.5 31.4 %all-to-all-done = bf16[32,64,256]{2,1,0:T(8,128)(2,1)S(1)} async-done(((bf16[32,64,256]{2,1,0:T(8,128)(2,1)}), bf16[32,64,256]{2,1,0:T(8,128)(2,1)S(1)}, u32[]{:S(2)}, u32[]{:S(2)}) %all-to-all-start) | async-done | bytes 1048608 | tf_op jit(solution)/shard_map/all_to_all | solution.py:14
  51.9 0.2 broadcast_in_dim.27
  52.2 8.1 %all_to_all.31 = bf16[2,32,64,256]{3,2,1,0:T(8,128)(2,1)S(1)} all-to-all(bf16[2,32,64,256]{3,2,1,0:T(8,128)(2,1)S(1)} %broadcast_in_dim.27), channel_id=1, replica_groups=mesh['dp_0'=8,'dp_1'=4,'dp_2'=2,'mp'=8] {'dp_2'}, dimensions={0} | all-to-all | bytes 4194304 | tf_op jit(solution)/shard_map/all_to_all | solution.py:14
  60.3 0.0 copy-start
  60.3 0.1 copy.9
  60.4 0.5 copy-done
  61.0 0.0 copy-start.1
  61.0 4.7 %while.24 = (s32[]{:T(128)}, f32[512]{0:T(512)S(1)}, f32[512]{0:T(512)S(1)}, s32[8,512]{1,0:T(8,128)S(1)}, bf16[8,512,256]{2,1,0:T(8,128)(2,1)S(1)}, /*index=5*/...) while((s32[]{:T(128)}, f32[512]{0:T(512)S(1)}, ...), condition=%wide.region_4.5_spmd.clone, body=%wide.region_1.4_spmd.clone.sunk | while | flops 136054272 | bytes 553083 | solution.py:121
  61.0 0.5 select_reduce_fusion.3
  61.6 0.5 select_reduce_fusion.3
  62.2 0.5 select_reduce_fusion.3
  62.8 0.5 select_reduce_fusion.3
  63.3 0.5 select_reduce_fusion.3
  63.9 0.5 select_reduce_fusion.3
  64.5 0.5 select_reduce_fusion.3
  65.1 0.5 select_reduce_fusion.3
  65.7 0.6 broadcast_in_dim.28
  66.3 4.0 %all-to-all-start.2 = ((f32[8,1,1024]{2,1,0:T(1,128)}), f32[8,1,1024]{2,1,0:T(1,128)S(1)}, u32[]{:S(2)}, u32[]{:S(2)}) async-start(f32[8,1,1024]{2,1,0:T(1,128)} %broadcast_in_dim.28), calls=%async_computation.2 | async-start | bytes 65536 | tf_op jit(solution)/shard_map/all_to_all | solution.py:14
  70.3 0.0 copy-done.1
  70.3 0.1 dynamic-slice_bitcast_fusion
  70.4 5.0 %all-to-all-done.2 = f32[8,1,1024]{2,1,0:T(1,128)S(1)} async-done(((f32[8,1,1024]{2,1,0:T(1,128)}), f32[8,1,1024]{2,1,0:T(1,128)S(1)}, u32[]{:S(2)}, u32[]{:S(2)}) %all-to-all-start.2) | async-done | bytes 32800 | tf_op jit(solution)/shard_map/all_to_all | solution.py:14
  75.5 0.6 slice_log_fusion
  76.1 0.1 dynamic-slice_bitcast_fusion.1
  76.2 0.7 reshape.68
  76.9 8.0 %all-to-all-start.3 = ((f32[64,1,128]{2,1,0:T(1,128)}), f32[64,1,128]{2,1,0:T(1,128)S(1)}, u32[]{:S(2)}, u32[]{:S(2)}) async-start(f32[64,1,128]{2,1,0:T(1,128)} %reshape.68), calls=%async_computation.3 | async-start | bytes 65536 | tf_op jit(solution)/shard_map/all_to_all | solution.py:51
  85.0 11.8 %all-to-all-done.3 = f32[64,1,128]{2,1,0:T(1,128)S(1)} async-done(((f32[64,1,128]{2,1,0:T(1,128)}), f32[64,1,128]{2,1,0:T(1,128)S(1)}, u32[]{:S(2)}, u32[]{:S(2)}) %all-to-all-start.3) | async-done | bytes 32800 | tf_op jit(solution)/shard_map/all_to_all | solution.py:51
  96.7 0.6 broadcast.107
  97.3 0.8 reduce.9
  98.1 0.1 reshape.69
  98.2 0.1 reshape.53
  98.3 0.1 slice_reduce_fusion
  98.4 22.0 %while.25 = (s32[]{:T(128)}, f32[512,256]{1,0:T(8,128)}, s32[8,512]{1,0:T(8,128)S(1)}, f32[512]{0:T(512)S(1)}, bf16[8,512,256]{2,1,0:T(8,128)(2,1)S(1)}, /*index...) while((s32[]{:T(128)}, f32[512,256]{1,0:T(8,128)}, ...), condition=%wide.region_7.8_spmd.clone, body=%wide.region_6.7_spmd.clone.sunk | while | flops 272105984 | bytes 1868947 | solution.py:142
  98.5 1.8 %convolution_add_fusion.2 = f32[512,256]{1,0:T(8,128)} fusion(bf16[512,256]{1,0:T(8,128)(2,1)S(1)} %get-tuple-element.413, f32[512,256]{1,0:T(8,128)} %get-tuple-element.396, f32[512]{0:T(512)S(1)} %bitcast.63, f32[512]{0:T(512)S(1)} %get-tuple-element.411, s32[512]{0:T(512)S(1)} %get-tuple-element.417, f32[512]{0:T(512)S(1)} %bitcast.62, ...), kind=kOutput, calls=%fused_computation.14.clone.1 | convolution fusion | flops 272105472 | bytes 1854465 | tf_op jit(solution)/shard_map/while/body/eval_jaxpr/dot_general | solution.py:139
  100.3 2.8 %convolution_add_fusion.2 = f32[512,256]{1,0:T(8,128)} fusion(bf16[512,256]{1,0:T(8,128)(2,1)S(1)} %get-tuple-element.413, f32[512,256]{1,0:T(8,128)} %get-tuple-element.396, f32[512]{0:T(512)S(1)} %bitcast.63, f32[512]{0:T(512)S(1)} %get-tuple-element.411, s32[512]{0:T(512)S(1)} %get-tuple-element.417, f32[512]{0:T(512)S(1)} %bitcast.62, ...), kind=kOutput, calls=%fused_computation.14.clone.1 | convolution fusion | flops 272105472 | bytes 1854465 | tf_op jit(solution)/shard_map/while/body/eval_jaxpr/dot_general | solution.py:139
  103.2 2.8 %convolution_add_fusion.2 = f32[512,256]{1,0:T(8,128)} fusion(bf16[512,256]{1,0:T(8,128)(2,1)S(1)} %get-tuple-element.413, f32[512,256]{1,0:T(8,128)} %get-tuple-element.396, f32[512]{0:T(512)S(1)} %bitcast.63, f32[512]{0:T(512)S(1)} %get-tuple-element.411, s32[512]{0:T(512)S(1)} %get-tuple-element.417, f32[512]{0:T(512)S(1)} %bitcast.62, ...), kind=kOutput, calls=%fused_computation.14.clone.1 | convolution fusion | flops 272105472 | bytes 1854465 | tf_op jit(solution)/shard_map/while/body/eval_jaxpr/dot_general | solution.py:139
  106.1 2.8 %convolution_add_fusion.2 = f32[512,256]{1,0:T(8,128)} fusion(bf16[512,256]{1,0:T(8,128)(2,1)S(1)} %get-tuple-element.413, f32[512,256]{1,0:T(8,128)} %get-tuple-element.396, f32[512]{0:T(512)S(1)} %bitcast.63, f32[512]{0:T(512)S(1)} %get-tuple-element.411, s32[512]{0:T(512)S(1)} %get-tuple-element.417, f32[512]{0:T(512)S(1)} %bitcast.62, ...), kind=kOutput, calls=%fused_computation.14.clone.1 | convolution fusion | flops 272105472 | bytes 1854465 | tf_op jit(solution)/shard_map/while/body/eval_jaxpr/dot_general | solution.py:139
  109.0 2.8 %convolution_add_fusion.2 = f32[512,256]{1,0:T(8,128)} fusion(bf16[512,256]{1,0:T(8,128)(2,1)S(1)} %get-tuple-element.413, f32[512,256]{1,0:T(8,128)} %get-tuple-element.396, f32[512]{0:T(512)S(1)} %bitcast.63, f32[512]{0:T(512)S(1)} %get-tuple-element.411, s32[512]{0:T(512)S(1)} %get-tuple-element.417, f32[512]{0:T(512)S(1)} %bitcast.62, ...), kind=kOutput, calls=%fused_computation.14.clone.1 | convolution fusion | flops 272105472 | bytes 1854465 | tf_op jit(solution)/shard_map/while/body/eval_jaxpr/dot_general | solution.py:139
  111.8 2.8 %convolution_add_fusion.2 = f32[512,256]{1,0:T(8,128)} fusion(bf16[512,256]{1,0:T(8,128)(2,1)S(1)} %get-tuple-element.413, f32[512,256]{1,0:T(8,128)} %get-tuple-element.396, f32[512]{0:T(512)S(1)} %bitcast.63, f32[512]{0:T(512)S(1)} %get-tuple-element.411, s32[512]{0:T(512)S(1)} %get-tuple-element.417, f32[512]{0:T(512)S(1)} %bitcast.62, ...), kind=kOutput, calls=%fused_computation.14.clone.1 | convolution fusion | flops 272105472 | bytes 1854465 | tf_op jit(solution)/shard_map/while/body/eval_jaxpr/dot_general | solution.py:139
  114.7 2.8 %convolution_add_fusion.2 = f32[512,256]{1,0:T(8,128)} fusion(bf16[512,256]{1,0:T(8,128)(2,1)S(1)} %get-tuple-element.413, f32[512,256]{1,0:T(8,128)} %get-tuple-element.396, f32[512]{0:T(512)S(1)} %bitcast.63, f32[512]{0:T(512)S(1)} %get-tuple-element.411, s32[512]{0:T(512)S(1)} %get-tuple-element.417, f32[512]{0:T(512)S(1)} %bitcast.62, ...), kind=kOutput, calls=%fused_computation.14.clone.1 | convolution fusion | flops 272105472 | bytes 1854465 | tf_op jit(solution)/shard_map/while/body/eval_jaxpr/dot_general | solution.py:139
  117.6 2.8 %convolution_add_fusion.2 = f32[512,256]{1,0:T(8,128)} fusion(bf16[512,256]{1,0:T(8,128)(2,1)S(1)} %get-tuple-element.413, f32[512,256]{1,0:T(8,128)} %get-tuple-element.396, f32[512]{0:T(512)S(1)} %bitcast.63, f32[512]{0:T(512)S(1)} %get-tuple-element.411, s32[512]{0:T(512)S(1)} %get-tuple-element.417, f32[512]{0:T(512)S(1)} %bitcast.62, ...), kind=kOutput, calls=%fused_computation.14.clone.1 | convolution fusion | flops 272105472 | bytes 1854465 | tf_op jit(solution)/shard_map/while/body/eval_jaxpr/dot_general | solution.py:139
  120.4 3.5 %all-to-all-start.4 = ((f32[8,64,256]{2,1,0:T(8,128)}), f32[8,64,256]{2,1,0:T(8,128)S(1)}, u32[]{:S(2)}, u32[]{:S(2)}) async-start(f32[8,64,256]{2,1,0:T(8,128)} %bitcast.5), calls=%async_computation.4 | async-start | bytes 1048576 | tf_op jit(solution)/shard_map/all_to_all | solution.py:70
  123.9 0.1 dynamic_slice.40
  124.0 8.1 %all-to-all-done.4 = f32[8,64,256]{2,1,0:T(8,128)S(1)} async-done(((f32[8,64,256]{2,1,0:T(8,128)}), f32[8,64,256]{2,1,0:T(8,128)S(1)}, u32[]{:S(2)}, u32[]{:S(2)}) %all-to-all-start.4) | async-done | bytes 524320 | tf_op jit(solution)/shard_map/all_to_all | solution.py:70
  132.1 0.1 multiply_reduce_fusion
  132.2 0.1 subtract_divide_fusion
  132.4 13.2 %all_to_all.32 = f32[8,64,256]{2,1,0:T(8,128)S(1)} all-to-all(f32[8,64,256]{2,1,0:T(8,128)S(1)} %broadcast_in_dim.30), channel_id=1, replica_groups=mesh['dp_0'=8,'dp_1'=4,'dp_2'=2,'mp'=8] {'mp'}, dimensions={0} | all-to-all | bytes 1048576 | tf_op jit(solution)/shard_map/all_to_all | solution.py:14
  145.6 0.8 copy.31
  (63 shorter events, 0.6 us)
Async XLA Ops:
  4.0 48.0 %all-to-all-start = ((bf16[32,64,256]{2,1,0:T(8,128)(2,1)}), bf16[32,64,256]{2,1,0:T(8,128)(2,1)S(1)}, u32[]{:S(2)}, u32[]{:S(2)}) async-start(bf16[32,64,256]{2,1,0:T(8,128)(2,1)} %broadcast_in_dim.26), calls=%async_computation | async-start | bytes 2097152 | tf_op jit(solution)/shard_map/all_to_all | solution.py:14
  60.3 0.7 copy-start
  61.0 9.4 %copy-start.1 = (f32[512]{0:T(512)S(1)}, f32[512]{0:T(512)}, u32[]{:S(2)}) copy-start(f32[512]{0:T(512)} %param.9) | copy-start | bytes 6148
  66.3 9.1 %all-to-all-start.2 = ((f32[8,1,1024]{2,1,0:T(1,128)}), f32[8,1,1024]{2,1,0:T(1,128)S(1)}, u32[]{:S(2)}, u32[]{:S(2)}) async-start(f32[8,1,1024]{2,1,0:T(1,128)} %broadcast_in_dim.28), calls=%async_computation.2 | async-start | bytes 65536 | tf_op jit(solution)/shard_map/all_to_all | solution.py:14
  76.9 19.9 %all-to-all-start.3 = ((f32[64,1,128]{2,1,0:T(1,128)}), f32[64,1,128]{2,1,0:T(1,128)S(1)}, u32[]{:S(2)}, u32[]{:S(2)}) async-start(f32[64,1,128]{2,1,0:T(1,128)} %reshape.68), calls=%async_computation.3 | async-start | bytes 65536 | tf_op jit(solution)/shard_map/all_to_all | solution.py:51
  120.4 11.7 %all-to-all-start.4 = ((f32[8,64,256]{2,1,0:T(8,128)}), f32[8,64,256]{2,1,0:T(8,128)S(1)}, u32[]{:S(2)}, u32[]{:S(2)}) async-start(f32[8,64,256]{2,1,0:T(8,128)} %bitcast.5), calls=%async_computation.4 | async-start | bytes 1048576 | tf_op jit(solution)/shard_map/all_to_all | solution.py:70
